TPU v7x, 256 devices: a whole 4x4x8 slice. The times are simulated.
256 devices in a mesh: pix: 16 (over x_hi, z), peak: 16 (over y, x_lo, core).
Axes of the slice: x: 4 (x_hi: 2, x_lo: 2; x = x_hi * 2 + x_lo), y: 4, z: 8, core: 2. Of those that a mesh axis runs over, the one named last changes fastest.
Arguments:
- cube: bfloat16 [65536, 8, 2048], P('pix', None, 'peak'), may hold values from -6 to 6
- pix_factor: bfloat16 [65536, 64], P(('pix', 'peak')), may hold values from -0.8984375 to 0.8984375
- sec_factor: bfloat16 [8, 64], replicated, may hold values from -5 to 5
- peak_factor: bfloat16 [2048, 64], P('peak'), may hold values from -0.046875 to 0.046875
Outputs:
- grad_pix: float32 [65536, 64], P(('pix', 'peak'))
- grad_peak: float32 [2048, 64], P('peak')
All inputs are finite; a program needn't handle non-finite values.
Results may differ from a plain program's by a relative error of at most 0.0003.
Values may be sent and summed in bfloat16 or wider, within the bound.
No kernel may reach another device: no remote copies, remote signals or barrier semaphores. Data moves between devices by JAX's collectives and lax.ppermute only.
A program may use at most 64 MiB of HBM per device.

v0:
```python
import math
import jax
import jax.numpy as jnp
from jax import lax
from jax.sharding import PartitionSpec as P


def on_device(cube, pix_factor, sec_factor, peak_factor):
    pixels = cube.shape[0]
    sections = cube.shape[1]
    peaks = cube.shape[2]
    rank = peak_factor.shape[1]
    fb = sec_factor.astype(jnp.float32)
    fa_own = pix_factor.astype(jnp.float32)
    fc_own = peak_factor.astype(jnp.float32)
    gathered = lax.all_gather(pix_factor, "peak", axis=0, tiled=True)
    ttm = jnp.dot(
        cube.reshape(pixels * sections, peaks), peak_factor, preferred_element_type=jnp.float32
    )
    ttm = ttm.reshape(pixels, sections, rank)
    summed_pix = lax.psum_scatter(
        jnp.sum(ttm * fb[None, :, :], axis=1), "peak", scatter_dimension=0, tiled=True
    )
    partial_peak = jnp.zeros((peaks, rank), jnp.float32)
    for index in range(sections):
        inner = lax.dot_general(
            cube[:, index, :],
            gathered,
            (((0,), (0,)), ((), ())),
            preferred_element_type=jnp.float32,
        )
        partial_peak = partial_peak + inner * fb[index][None, :]
    local_a = jnp.dot(pix_factor.T, pix_factor, preferred_element_type=jnp.float32)
    local_c = jnp.dot(peak_factor.T, peak_factor, preferred_element_type=jnp.float32)
    gram_b = jnp.dot(sec_factor.T, sec_factor, preferred_element_type=jnp.float32)
    gram_a = lax.psum(local_a, ("pix", "peak"))
    gram_c = lax.psum(local_c, "peak")
    grad_pix = summed_pix - jnp.dot(fa_own, gram_b * gram_c, precision=lax.Precision.HIGHEST)
    scale = 1.0 / math.sqrt(float(sections * pixels * lax.axis_size("pix")))
    weight_c = gram_a * gram_b
    total = lax.psum(partial_peak, "pix")
    grad_peak = (total - jnp.dot(fc_own, weight_c, precision=lax.Precision.HIGHEST)) * scale
    return (grad_pix, grad_peak)


def solution(mesh):
    in_specs = (P("pix", None, "peak"), P(("pix", "peak"), None), P(), P("peak", None))
    out_specs = (P(("pix", "peak"), None), P("peak", None))
    return jax.shard_map(
        on_device, mesh=mesh, in_specs=in_specs, out_specs=out_specs, check_vma=False
    )
```

profile of v0, /device:TPU:4, one launch (start us, length us, event | category | flops | bytes accessed | tf_op | source)
XLA Modules:
  0.0 273.6 jit_solution(18076057092134265733)
XLA Ops:
  7.2 0.0 copy-start
  7.2 0.0 reduce-scatter.2.cloned.1.call-start
  7.2 0.7 convert_element_type.2
  7.9 0.0 copy-done
  7.9 7.9 %multiply_reduce_fusion = f32[4096,64]{0,1:T(8,128)} fusion(f32[8,64]{1,0:T(8,128)S(1)} %convert_element_type.2, bf16[128,64]{0,1:T(8,128)(2,1)S(1)} %copy-done, bf16[4096,8,128]{2,1,0:T(8,128)(2,1)} %param.4), kind=kOutput, calls=%fused_computation | convolution fusion | flops 540803072 | bytes 9455616 | tf_op jit(solution)/shard_map/dot_general | solution.py:17
  15.9 0.0 reduce-scatter.2.cloned.1.call-update
  15.9 0.0 copy-start.1
  15.9 7.7 %copy.7 = bf16[4096,8,128]{2,0,1:T(8,128)(2,1)} copy(bf16[4096,8,128]{2,1,0:T(8,128)(2,1)} %param.4) | data formatting | bytes 16777216 | tf_op args[0]
  23.6 0.0 copy-done.1
  23.6 0.0 copy-start.2
  23.6 23.0 %all_gather.3 = bf16[4096,64]{0,1:T(8,128)(2,1)S(1)} all-gather(bf16[256,64]{0,1:T(8,128)(2,1)S(1)} %copy-done.1), channel_id=1, replica_groups=mesh['pix'=16,'peak'=16] {'peak'}, dimensions={0}, use_global_device_ids=true | all-gather | bytes 557056 | tf_op jit(solution)/shard_map/all_gather | solution.py:16
  46.6 0.1 fusion.16
  46.7 0.1 fusion.15
  46.8 1.6 convolution_multiply_fusion.7
  48.4 1.5 fusion.7
  50.0 77.0 %psum.23 = f32[64,64]{1,0:T(8,128)S(1)} all-reduce(f32[64,64]{1,0:T(8,128)S(1)} %fusion.16), channel_id=1, replica_groups=mesh['pix'=16,'peak'=16] {'pix','peak'}, use_global_device_ids=true, to_apply=%region_4.0 | all-reduce | flops 4096 | bytes 32768 | tf_op jit(solution)/shard_map/psum | solution.py:36
  126.9 53.7 %psum.21 = f32[64,64]{1,0:T(8,128)S(1)} all-reduce(f32[64,64]{1,0:T(8,128)S(1)} %fusion.15), channel_id=1, replica_groups=mesh['pix'=16,'peak'=16] {'peak'}, use_global_device_ids=true, to_apply=%region_2.0 | all-reduce | flops 4096 | bytes 32768 | tf_op jit(solution)/shard_map/psum | solution.py:37
  180.6 1.5 fusion.6
  182.2 1.5 fusion.5
  183.7 1.5 fusion.4
  185.3 1.5 fusion.3
  186.8 1.5 fusion.2
  188.3 1.5 fusion.1
  189.9 74.1 %psum.22 = f32[128,64]{0,1:T(8,128)S(1)} all-reduce(f32[128,64]{0,1:T(8,128)S(1)} %fusion.1), channel_id=1, replica_groups=mesh['pix'=16,'peak'=16] {'pix'}, use_global_device_ids=true, to_apply=%region_3.0 | all-reduce | flops 8192 | bytes 65536 | tf_op jit(solution)/shard_map/psum | solution.py:41
  264.0 0.0 copy-done.2
  264.0 0.2 fusion.14
  264.2 0.8 fusion.9
  265.1 0.0 reduce-scatter.2.cloned.1.call-done
  265.1 1.7 fusion
  (1 shorter events, 0.0 us)
Async XLA Ops:
  7.2 0.8 copy-start
  7.2 257.9 %reduce-scatter.2.cloned.1.call-start = ((), (), s32[]{:S(2)}) async-start(), calls=%async_computation.1 | async-start | bytes 1114112 | tf_op jit(solution)/shard_map/reduce_scatter | solution.py:21
  15.9 7.7 %copy-start.1 = (bf16[256,64]{0,1:T(8,128)(2,1)S(1)}, bf16[256,64]{0,1:T(8,128)(2,1)}, u32[]{:S(2)}) copy-start(bf16[256,64]{0,1:T(8,128)(2,1)} %param.5) | copy-start | bytes 98308
  23.6 240.4 %copy-start.2 = (bf16[8,64]{1,0:T(8,128)(2,1)S(1)}, bf16[8,64]{1,0:T(8,128)(2,1)}, u32[]{:S(2)}) copy-start(bf16[8,64]{1,0:T(8,128)(2,1)} %param.6) | copy-start | bytes 3076
Sparse Core Ops, SparseCore 0:
  16.0 66.9 reduce-scatter.1
where the time goes:
time: 274 us
  blocking collectives  228 us (83%)
  matrix products  23.3 us (9%)
  between operations  14.1 us (5%)
  local copies, waits for them, and re-layouts  7.72 us (3%)
    psum x1, blocking collectives, on_device(): gram_a = lax.psum(local_a, ('pix', 'peak'))  77 us
    psum x1, blocking collectives, on_device(): total = lax.psum(partial_peak, 'pix')  74.1 us
    psum x1, blocking collectives, on_device(): gram_c = lax.psum(local_c, 'peak')  53.7 us
    all_gather x1, blocking collectives, on_device(): gathered = lax.all_gather(pix_factor, 'peak', axis=0, tiled=True)  23 us
    dot_general x8, matrix products, on_device(): lax.dot_general(cube[:, index, :], gathered, (((0,), (0,)), ((), ())), pr...  12.4 us
    dot_general x1, matrix products, on_device(): jnp.dot(cube.reshape(pixels * sections, peaks), peak_factor, preferred_el...  7.95 us
    unnamed x7, local copies, waits for them, and re-layouts  7.71 us
  transfers between devices with their start and end apart: 1, of which 0 were waited for; matrix products, arithmetic and copies ran while one was open for 8% of the time, Pallas kernels for 0%

commit v1 on v0

--- a/solution.py
+++ b/solution.py
@@ -33,7 +33,7 @@
     local_a = jnp.dot(pix_factor.T, pix_factor, preferred_element_type=jnp.float32)
     local_c = jnp.dot(peak_factor.T, peak_factor, preferred_element_type=jnp.float32)
     gram_b = jnp.dot(sec_factor.T, sec_factor, preferred_element_type=jnp.float32)
-    gram_a = lax.psum(local_a, ("pix", "peak"))
+    gram_a = lax.psum(lax.psum(local_a, "peak"), "pix")
     gram_c = lax.psum(local_c, "peak")
     grad_pix = summed_pix - jnp.dot(fa_own, gram_b * gram_c, precision=lax.Precision.HIGHEST)
     scale = 1.0 / math.sqrt(float(sections * pixels * lax.axis_size("pix")))

time: 274 us -> 200 us (0.73)
  blocking collectives: 228 us -> 153 us
    psum x1 -> x0, blocking collectives: 77 us -> none  [on_device(): gram_a = lax.psum(local_a, ('pix', 'peak'))]
    psum x1, blocking collectives: 74.1 us -> 76.9 us  [on_device(): total = lax.psum(partial_peak, 'pix')]
  transfers between devices with their start and end apart: 1 -> 1, of which waited for: 0 -> 0; matrix products, arithmetic and copies ran while one was open for 8% -> 11% of each run, Pallas kernels for 0% -> 0%
where the time goes in v1:
time: 200 us; the launch traced here: 199 us
  blocking collectives  153 us (76%)
  matrix products  23.3 us (12%)
  between operations  14.1 us (7%)
  local copies, waits for them, and re-layouts  7.72 us (4%)
    psum x1, blocking collectives, on_device(): total = lax.psum(partial_peak, 'pix')  76.9 us
    psum x1, blocking collectives, on_device(): gram_c = lax.psum(local_c, 'peak')  53.2 us
    all_gather x1, blocking collectives, on_device(): gathered = lax.all_gather(pix_factor, 'peak', axis=0, tiled=True)  23 us
    dot_general x8, matrix products, on_device(): lax.dot_general(cube[:, index, :], gathered, (((0,), (0,)), ((), ())), pr...  12.3 us
    dot_general x1, matrix products, on_device(): jnp.dot(cube.reshape(pixels * sections, peaks), peak_factor, preferred_el...  7.95 us
    unnamed x7, local copies, waits for them, and re-layouts  7.71 us
  transfers between devices with their start and end apart: 1, of which 0 were waited for; matrix products, arithmetic and copies ran while one was open for 11% of the time, Pallas kernels for 0%

profile of v1, /device:TPU:4, one launch (start us, length us, event | category | flops | bytes accessed | tf_op | source)
XLA Modules:
  0.0 199.0 jit_solution(11312229132398940934)
XLA Ops:
  7.2 0.0 copy-start
  7.2 0.0 reduce-scatter.2.cloned.1.call-start
  7.2 0.7 convert_element_type.2
  7.9 0.0 copy-done
  7.9 7.9 %multiply_reduce_fusion = f32[4096,64]{0,1:T(8,128)} fusion(f32[8,64]{1,0:T(8,128)S(1)} %convert_element_type.2, bf16[128,64]{0,1:T(8,128)(2,1)S(1)} %copy-done, bf16[4096,8,128]{2,1,0:T(8,128)(2,1)} %param.4), kind=kOutput, calls=%fused_computation | convolution fusion | flops 540803072 | bytes 9455616 | tf_op jit(solution)/shard_map/dot_general | solution.py:17
  15.9 0.0 reduce-scatter.2.cloned.1.call-update
  15.9 0.0 copy-start.1
  15.9 7.7 %copy.7 = bf16[4096,8,128]{2,0,1:T(8,128)(2,1)} copy(bf16[4096,8,128]{2,1,0:T(8,128)(2,1)} %param.4) | data formatting | bytes 16777216 | tf_op args[0]
  23.6 0.0 copy-done.1
  23.6 0.0 copy-start.2
  23.6 23.0 %all_gather.3 = bf16[4096,64]{0,1:T(8,128)(2,1)S(1)} all-gather(bf16[256,64]{0,1:T(8,128)(2,1)S(1)} %copy-done.1), channel_id=1, replica_groups=mesh['pix'=16,'peak'=16] {'peak'}, dimensions={0}, use_global_device_ids=true | all-gather | bytes 557056 | tf_op jit(solution)/shard_map/all_gather | solution.py:16
  46.6 0.1 fusion.16
  46.7 1.6 convolution_multiply_fusion.7
  48.3 1.5 fusion.7
  49.8 0.1 fusion.15
  49.9 53.2 %all-reduce = (f32[64,64]{1,0:T(8,128)S(1)}, f32[64,64]{1,0:T(8,128)S(1)}) all-reduce(f32[64,64]{1,0:T(8,128)S(1)} %fusion.15, f32[64,64]{1,0:T(8,128)S(1)} %fusion.16), channel_id=1, replica_groups=mesh['pix'=16,'peak'=16] {'peak'}, use_global_device_ids=true, to_apply=%region_2.0 | all-reduce | flops 8192 | bytes 65536 | tf_op jit(solution)/shard_map/psum | solution.py:37
  103.2 1.5 fusion.6
  104.7 1.5 fusion.5
  106.3 1.5 fusion.4
  107.8 1.5 fusion.3
  109.4 1.5 fusion.2
  110.9 1.5 fusion.1
  112.5 76.9 %all-reduce.1 = (f32[128,64]{0,1:T(8,128)S(1)}, f32[64,64]{1,0:T(8,128)S(1)}) all-reduce(f32[128,64]{0,1:T(8,128)S(1)} %fusion.1, f32[64,64]{1,0:T(8,128)S(1)} %get-tuple-element.3), channel_id=1, replica_groups=mesh['pix'=16,'peak'=16] {'pix'}, use_global_device_ids=true, to_apply=%region_3.0 | all-reduce | flops 12288 | bytes 98304 | tf_op jit(solution)/shard_map/psum | solution.py:41
  189.4 0.0 copy-done.2
  189.4 0.2 fusion.14
  189.6 0.8 fusion.9
  190.4 0.0 reduce-scatter.2.cloned.1.call-done
  190.4 1.7 fusion
  (1 shorter events, 0.0 us)
Async XLA Ops:
  7.2 0.8 copy-start
  7.2 183.2 %reduce-scatter.2.cloned.1.call-start = ((), (), s32[]{:S(2)}) async-start(), calls=%async_computation.1 | async-start | bytes 1114112 | tf_op jit(solution)/shard_map/reduce_scatter | solution.py:21
  15.9 7.7 %copy-start.1 = (bf16[256,64]{0,1:T(8,128)(2,1)S(1)}, bf16[256,64]{0,1:T(8,128)(2,1)}, u32[]{:S(2)}) copy-start(bf16[256,64]{0,1:T(8,128)(2,1)} %param.5) | copy-start | bytes 98308
  23.6 165.8 %copy-start.2 = (bf16[8,64]{1,0:T(8,128)(2,1)S(1)}, bf16[8,64]{1,0:T(8,128)(2,1)}, u32[]{:S(2)}) copy-start(bf16[8,64]{1,0:T(8,128)(2,1)} %param.6) | copy-start | bytes 3076
Sparse Core Ops, SparseCore 0:
  16.0 66.7 reduce-scatter.1

commit v2 on v0

--- a/solution.py
+++ b/solution.py
@@ -34,7 +34,7 @@
     local_c = jnp.dot(peak_factor.T, peak_factor, preferred_element_type=jnp.float32)
     gram_b = jnp.dot(sec_factor.T, sec_factor, preferred_element_type=jnp.float32)
     gram_a = lax.psum(local_a, ("pix", "peak"))
-    gram_c = lax.psum(local_c, "peak")
+    gram_c = jnp.sum(lax.all_gather(local_c, "peak"), axis=0)
     grad_pix = summed_pix - jnp.dot(fa_own, gram_b * gram_c, precision=lax.Precision.HIGHEST)
     scale = 1.0 / math.sqrt(float(sections * pixels * lax.axis_size("pix")))
     weight_c = gram_a * gram_b

time: 274 us -> 241 us (0.88)
  blocking collectives: 228 us -> 194 us
    psum x1 -> x0, blocking collectives: 53.7 us -> none  [on_device(): gram_c = lax.psum(local_c, 'peak')]
    all_gather x0 -> x1, blocking collectives: none -> 19.1 us  [on_device(): gram_c = jnp.sum(lax.all_gather(local_c, 'peak'), axis=0)]
  transfers between devices with their start and end apart: 1 -> 1, of which waited for: 0 -> 0; matrix products, arithmetic and copies ran while one was open for 8% -> 9% of each run, Pallas kernels for 0% -> 0%
where the time goes in v2:
time: 241 us; the launch traced here: 240 us
  blocking collectives  194 us (80%)
  matrix products  23.3 us (10%)
  between operations  14.1 us (6%)
  local copies, waits for them, and re-layouts  7.72 us (3%)
    psum x1, blocking collectives, on_device(): gram_a = lax.psum(local_a, ('pix', 'peak'))  76.8 us
    psum x1, blocking collectives, on_device(): total = lax.psum(partial_peak, 'pix')  75 us
    all_gather x1, blocking collectives, on_device(): gathered = lax.all_gather(pix_factor, 'peak', axis=0, tiled=True)  23 us
    all_gather x1, blocking collectives, on_device(): gram_c = jnp.sum(lax.all_gather(local_c, 'peak'), axis=0)  19.1 us
    dot_general x8, matrix products, on_device(): lax.dot_general(cube[:, index, :], gathered, (((0,), (0,)), ((), ())), pr...  12.3 us
    dot_general x1, matrix products, on_device(): jnp.dot(cube.reshape(pixels * sections, peaks), peak_factor, preferred_el...  7.95 us
    unnamed x7, local copies, waits for them, and re-layouts  7.71 us
  transfers between devices with their start and end apart: 1, of which 0 were waited for; matrix products, arithmetic and copies ran while one was open for 9% of the time, Pallas kernels for 0%

profile of v2, /device:TPU:4, one launch (start us, length us, event | category | flops | bytes accessed | tf_op | source)
XLA Modules:
  0.0 239.7 jit_solution(1521257946146376661)
XLA Ops:
  7.2 0.0 copy-start
  7.2 0.0 reduce-scatter.2.cloned.1.call-start
  7.2 0.7 convert_element_type.2
  7.9 0.0 copy-done
  7.9 7.9 %multiply_reduce_fusion = f32[4096,64]{0,1:T(8,128)} fusion(f32[8,64]{1,0:T(8,128)S(1)} %convert_element_type.2, bf16[128,64]{0,1:T(8,128)(2,1)S(1)} %copy-done, bf16[4096,8,128]{2,1,0:T(8,128)(2,1)} %param.4), kind=kOutput, calls=%fused_computation | convolution fusion | flops 540803072 | bytes 9455616 | tf_op jit(solution)/shard_map/dot_general | solution.py:17
  15.9 0.0 reduce-scatter.2.cloned.1.call-update
  15.9 0.0 copy-start.1
  15.9 7.7 %copy.7 = bf16[4096,8,128]{2,0,1:T(8,128)(2,1)} copy(bf16[4096,8,128]{2,1,0:T(8,128)(2,1)} %param.4) | data formatting | bytes 16777216 | tf_op args[0]
  23.6 0.0 copy-done.1
  23.6 0.0 copy-start.2
  23.6 23.0 %all_gather.11 = bf16[4096,64]{0,1:T(8,128)(2,1)S(1)} all-gather(bf16[256,64]{0,1:T(8,128)(2,1)S(1)} %copy-done.1), channel_id=1, replica_groups=mesh['pix'=16,'peak'=16] {'peak'}, dimensions={0}, use_global_device_ids=true | all-gather | bytes 557056 | tf_op jit(solution)/shard_map/all_gather | solution.py:16
  46.6 0.1 fusion.16
  46.7 0.1 fusion.15
  46.8 1.6 convolution_multiply_fusion.7
  48.4 1.5 fusion.7
  50.0 19.1 %all-gather = f32[1024,64]{1,0:T(8,128)S(1)} all-gather(f32[64,64]{1,0:T(8,128)S(1)} %fusion.15), channel_id=2, replica_groups=mesh['pix'=16,'peak'=16] {'peak'}, dimensions={0}, use_global_device_ids=true | all-gather | bytes 278528 | tf_op jit(solution)/shard_map/all_gather | solution.py:37
  69.1 76.8 %psum.15 = f32[64,64]{1,0:T(8,128)S(1)} all-reduce(f32[64,64]{1,0:T(8,128)S(1)} %fusion.16), channel_id=1, replica_groups=mesh['pix'=16,'peak'=16] {'pix','peak'}, use_global_device_ids=true, to_apply=%region_4.0 | all-reduce | flops 4096 | bytes 32768 | tf_op jit(solution)/shard_map/psum | solution.py:36
  145.9 1.5 fusion.6
  147.4 1.5 fusion.5
  149.0 1.5 fusion.4
  150.5 1.5 fusion.3
  152.1 1.5 fusion.2
  153.6 1.5 fusion.1
  155.2 75.0 %psum.14 = f32[128,64]{0,1:T(8,128)S(1)} all-reduce(f32[128,64]{0,1:T(8,128)S(1)} %fusion.1), channel_id=1, replica_groups=mesh['pix'=16,'peak'=16] {'pix'}, use_global_device_ids=true, to_apply=%region_3.0 | all-reduce | flops 8192 | bytes 65536 | tf_op jit(solution)/shard_map/psum | solution.py:41
  230.1 0.0 copy-done.2
  230.1 0.2 fusion.14
  230.3 0.8 fusion.9
  231.2 0.0 reduce-scatter.2.cloned.1.call-done
  231.2 1.7 fusion
  (2 shorter events, 0.1 us)
Async XLA Ops:
  7.2 0.8 copy-start
  7.2 224.0 %reduce-scatter.2.cloned.1.call-start = ((), (), s32[]{:S(2)}) async-start(), calls=%async_computation.1 | async-start | bytes 1114112 | tf_op jit(solution)/shard_map/reduce_scatter | solution.py:21
  15.9 7.7 %copy-start.1 = (bf16[256,64]{0,1:T(8,128)(2,1)S(1)}, bf16[256,64]{0,1:T(8,128)(2,1)}, u32[]{:S(2)}) copy-start(bf16[256,64]{0,1:T(8,128)(2,1)} %param.5) | copy-start | bytes 98308
  23.6 206.5 %copy-start.2 = (bf16[8,64]{1,0:T(8,128)(2,1)S(1)}, bf16[8,64]{1,0:T(8,128)(2,1)}, u32[]{:S(2)}) copy-start(bf16[8,64]{1,0:T(8,128)(2,1)} %param.6) | copy-start | bytes 3076
Sparse Core Ops, SparseCore 0:
  16.0 66.9 reduce-scatter.1
